TPU v7x, 512 devices: a whole 4x8x8 slice. The times are simulated.
512 devices in a mesh: row: 32 (over z_lo, x, core), col: 16 (over z_hi, y).
Axes of the slice: x: 4, y: 8, z: 8 (z_hi: 2, z_lo: 4; z = z_hi * 4 + z_lo), core: 2. Of those that a mesh axis runs over, the one named last changes fastest.
Arguments:
- state: float32 [32, 2, 16, 256, 256], P('row', None, 'col'), may hold values from -6 to 6
- a_tiles: float32 [32, 2, 16, 256, 256], P('row', None, 'col'), may hold values from -0.375 to 0.375
- inverses: float32 [32, 256, 256], P('row'), may hold values from -0.225 to 1.025
Outputs:
- state_out: float32 [32, 2, 16, 256, 256], P('row', None, 'col')
All inputs are finite; a program needn't handle non-finite values.
Results may differ from a plain program's by a relative error of at most 0.0001.
Values sent between devices are 32-bit elements; how exact they have to be, the bound alone decides.
A program may use at most 64 MiB of HBM per device.

v0:
```python
import jax
import jax.numpy as jnp
from jax import lax
from jax.sharding import PartitionSpec as P

FRONTS = 3
DOUBLINGS = 5
HIGH = lax.Precision.HIGHEST
shift_half = 0.5


def swapped(value, axis, stride):
    mask = 2**stride
    pairs = [(source, source ^ mask) for source in range(lax.axis_size(axis))]
    return lax.ppermute(value, axis, pairs)


def passed_along(block, axis, distance):
    devices = range(lax.axis_size(axis))
    route = [((i - distance) % len(devices), i) for i in devices]
    return lax.ppermute(block, axis, route)


def spread(value, axis, source):
    kept = jnp.where(lax.axis_index(axis) == source, value, 0).astype(value.dtype)
    return lax.psum(kept, axis)


def product(left, right):
    return jnp.dot(left, right, precision=HIGH, preferred_element_type=jnp.float32)


def product_transposed(left, right):
    return lax.dot_general(
        left, right, (((1,), (1,)), ((), ())), precision=HIGH, preferred_element_type=jnp.float32
    )


def batched_product(left, right):
    return jnp.einsum(
        "nab,nbc->nac", left, right, precision=HIGH, preferred_element_type=jnp.float32
    )


def across_cols(pieces):
    return lax.all_to_all(pieces, "col", split_axis=1, concat_axis=1, tiled=True)


def mirrored(tile_set):
    slot_count = tile_set.shape[0]
    tile_order = tile_set.shape[1]
    col_count = lax.axis_size("col")
    slab_rows = tile_order // col_count
    section_one = across_cols(tile_set.reshape(slot_count, col_count, slab_rows, tile_order))
    by_target = section_one.reshape(slot_count * col_count, slab_rows, tile_order)
    section_two = lax.all_to_all(by_target, "row", split_axis=0, concat_axis=0, tiled=True)
    section_three = across_cols(section_two.reshape(slot_count, col_count, slab_rows, tile_order))
    return section_three.reshape(slot_count, tile_order, tile_order)


def flipped(tile_set, col_count):
    levels = col_count.bit_length() - 1
    for bit_pos in range(levels):
        tile_set = swapped(tile_set, "col", bit_pos)
    return tile_set


def per_device(state, a_tiles, inverses):
    slot_count = state.shape[1]
    tile_order = state.shape[3]
    col_count = lax.axis_size("col")
    height = lax.axis_size("row")
    row_here = lax.axis_index("row")
    col_here = lax.axis_index("col")
    current = state.reshape(slot_count, tile_order, tile_order)
    coupling = a_tiles.reshape(slot_count, tile_order, tile_order)
    own_inverse = inverses.reshape(tile_order, tile_order)
    identity_tile = jnp.eye(tile_order, dtype=jnp.float32)
    left_powers = [identity_tile - shift_half * own_inverse]
    for level in range(DOUBLINGS - 1):
        left_powers.append(product(left_powers[-1], left_powers[-1]))
    column_inverse = mirrored(jnp.broadcast_to(own_inverse, (slot_count, tile_order, tile_order)))
    right_list = [identity_tile[None] - shift_half * column_inverse]
    for level in range(DOUBLINGS - 1):
        right_list.append(batched_product(right_list[-1], right_list[-1]))
    right_powers = jnp.stack(right_list)
    tile_cols = jnp.arange(slot_count, dtype=jnp.int32) * col_count + col_here
    tile_sum = row_here + tile_cols
    for front_step in range(FRONTS):
        front_sum = height - 1 - front_step
        source_a = flipped(coupling, col_count)
        if front_step > 0:
            source_a = passed_along(source_a, "col", -front_step)
        front_col = front_sum - row_here
        front_slot = jnp.clip(front_col // col_count, 0, slot_count - 1)
        own_tile = lax.dynamic_index_in_dim(current, front_slot, 0, keepdims=False)
        mirror = mirrored(current)
        far_tile = lax.dynamic_index_in_dim(mirror, front_slot, 0, keepdims=False)
        right_side = own_tile + far_tile.T
        right_inverse = lax.dynamic_index_in_dim(column_inverse, front_slot, 0, keepdims=False)
        powers_here = lax.dynamic_index_in_dim(right_powers, front_slot, 1, keepdims=False)
        solution = shift_half * product_transposed(product(own_inverse, right_side), right_inverse)
        for level in range(DOUBLINGS):
            solution = solution + product_transposed(
                product(left_powers[level], solution), powers_here[level]
            )
        passed = []
        for slot_pos in range(slot_count):
            root_row = jnp.clip(front_sum - tile_cols[slot_pos], 0, height - 1)
            passed.append(spread(solution, "row", root_row))
        below_rows = front_sum - tile_cols
        a_slot = jnp.clip(below_rows // col_count, 0, slot_count - 1)
        a_pick = jnp.take(source_a, a_slot, axis=0)
        update = batched_product(a_pick, jnp.stack(passed))
        shrink = (tile_sum < front_sum)[:, None, None]
        place = (tile_sum == front_sum)[:, None, None]
        current = jnp.where(shrink, current - update, jnp.where(place, solution[None], current))
    return current.reshape(state.shape)


def solution(mesh):
    in_specs = (
        P("row", None, "col", None, None),
        P("row", None, "col", None, None),
        P("row", None, None),
    )
    out_specs = P("row", None, "col", None, None)
    return jax.shard_map(
        per_device, mesh=mesh, in_specs=in_specs, out_specs=out_specs, check_vma=False
    )
```

profile of v0, /device:TPU:1, one launch (start us, length us, event | category | flops | bytes accessed | tf_op | source)
XLA Modules:
  0.0 1221.0 jit_solution(3985047102242037960)
XLA Ops:
  7.6 34.1 %all_to_all.60 = f32[2,16,16,256]{3,2,0,1:T(8,128)S(1)} all-to-all(f32[2,16,16,256]{3,2,0,1:T(8,128)S(1)} %copy.25), channel_id=1, replica_groups=mesh['row'=32,'col'=16] {'col'}, dimensions={1} | all-to-all | bytes 1048576 | tf_op jit(solution)/shard_map/all_to_all | solution.py:46
  50.0 16.1 %all-to-all-done.3 = f32[2,16,16,256]{3,2,0,1:T(8,128)S(1)} async-done(((f32[2,16,16,256]{3,2,0,1:T(8,128)}), f32[2,16,16,256]{3,2,0,1:T(8,128)S(1)}, u32[]{:S(2)}, u32[]{:S(2)}) %all-to-all-start.3) | async-done | bytes 524320 | tf_op jit(solution)/shard_map/all_to_all | solution.py:46
  66.1 10.6 all-to-all-start.1
  77.6 15.6 %all-to-all-done.1 = f32[32,16,256]{2,1,0:T(8,128)S(1)} async-done(((f32[32,16,256]{2,1,0:T(8,128)}), f32[32,16,256]{2,1,0:T(8,128)S(1)}, u32[]{:S(2)}, u32[]{:S(2)}) %all-to-all-start.1) | async-done | bytes 524320 | tf_op jit(solution)/shard_map/all_to_all | solution.py:56
  101.4 12.4 %all-to-all-done.4 = f32[32,16,256]{2,1,0:T(8,128)S(1)} async-done(((f32[32,16,256]{2,1,0:T(8,128)}), f32[32,16,256]{2,1,0:T(8,128)S(1)}, u32[]{:S(2)}, u32[]{:S(2)}) %all-to-all-start.4) | async-done | bytes 524320 | tf_op jit(solution)/shard_map/all_to_all | solution.py:56
  124.1 13.2 %all-to-all-done.2 = f32[2,16,16,256]{3,2,0,1:T(8,128)S(1)} async-done(((f32[2,16,16,256]{3,2,0,1:T(8,128)}), f32[2,16,16,256]{3,2,0,1:T(8,128)S(1)}, u32[]{:S(2)}, u32[]{:S(2)}) %all-to-all-start.2) | async-done | bytes 524320 | tf_op jit(solution)/shard_map/all_to_all | solution.py:46
  137.4 5.7 all-to-all-start.5
  143.8 15.3 %collective-permute-done.1 = f32[2,256,256]{2,1,0:T(8,128)} collective-permute-done((f32[2,256,256]{2,1,0:T(8,128)}, f32[2,256,256]{2,1,0:T(8,128)}, u32[]{:S(2)}, u32[]{:S(2)}) %collective-permute-start.1) | collective-permute-done | bytes 524320 | tf_op jit(solution)/shard_map/ppermute | solution.py:15
  159.0 8.0 collective-permute-start.2
  169.1 20.2 %collective-permute-done.2 = f32[2,256,256]{2,1,0:T(8,128)} collective-permute-done((f32[2,256,256]{2,1,0:T(8,128)}, f32[2,256,256]{2,1,0:T(8,128)}, u32[]{:S(2)}, u32[]{:S(2)}) %collective-permute-start.2) | collective-permute-done | bytes 524320 | tf_op jit(solution)/shard_map/ppermute | solution.py:15
  200.8 11.9 collective-permute-done.3
  215.1 269.7 %all-reduce.11.cloned.1.call-done = (f32[1,256,256]{2,1,0:T(8,128)}, f32[1,256,256]{2,1,0:T(8,128)}) async-done(((f32[1,256,256]{2,1,0:T(8,128)}, f32[1,256,256]{2,1,0:T(8,128)}), (f32[1,256,256]{2,1,0:T(8,128)}, f32[1,256,256]{2,1,0:T(8,128)})) %all-reduce.11.cloned.1.call-update) | async-done | bytes 524304 | tf_op jit(solution)/shard_map/psum | solution.py:26
  486.7 26.0 %all_to_all.61 = f32[2,16,16,256]{3,2,0,1:T(8,128)S(1)} all-to-all(f32[2,16,16,256]{3,2,0,1:T(8,128)S(1)} %copy.34), channel_id=1, replica_groups=mesh['row'=32,'col'=16] {'col'}, dimensions={1} | all-to-all | bytes 1048576 | tf_op jit(solution)/shard_map/all_to_all | solution.py:46
  512.8 23.9 %all_to_all.62 = f32[32,16,256]{2,1,0:T(8,128)S(1)} all-to-all(f32[32,16,256]{2,1,0:T(8,128)S(1)} %bitcast.223), channel_id=1, replica_groups=mesh['row'=32,'col'=16] {'row'}, dimensions={0} | all-to-all | bytes 1048576 | tf_op jit(solution)/shard_map/all_to_all | solution.py:56
  543.8 9.5 collective-permute-start.4
  553.3 8.2 all-to-all-done.8
  568.1 9.1 collective-permute-done.4
  579.5 270.4 %all-reduce.9.cloned.1.call-done = (f32[1,256,256]{2,1,0:T(8,128)}, f32[1,256,256]{2,1,0:T(8,128)}) async-done(((f32[1,256,256]{2,1,0:T(8,128)}, f32[1,256,256]{2,1,0:T(8,128)}), (f32[1,256,256]{2,1,0:T(8,128)}, f32[1,256,256]{2,1,0:T(8,128)})) %all-reduce.9.cloned.1.call-update) | async-done | bytes 524304 | tf_op jit(solution)/shard_map/psum | solution.py:26
  851.9 26.0 %all_to_all.63 = f32[2,16,16,256]{3,2,0,1:T(8,128)S(1)} all-to-all(f32[2,16,16,256]{3,2,0,1:T(8,128)S(1)} %copy.39), channel_id=1, replica_groups=mesh['row'=32,'col'=16] {'col'}, dimensions={1} | all-to-all | bytes 1048576 | tf_op jit(solution)/shard_map/all_to_all | solution.py:46
  878.0 23.9 %all_to_all.64 = f32[32,16,256]{2,1,0:T(8,128)S(1)} all-to-all(f32[32,16,256]{2,1,0:T(8,128)S(1)} %bitcast.225), channel_id=1, replica_groups=mesh['row'=32,'col'=16] {'row'}, dimensions={0} | all-to-all | bytes 1048576 | tf_op jit(solution)/shard_map/all_to_all | solution.py:56
  909.0 10.5 collective-permute-start.5
  919.4 7.3 all-to-all-done.11
  933.3 11.4 collective-permute-done.5
  945.3 266.6 %all-reduce.7.cloned.1.call-done = (f32[1,256,256]{2,1,0:T(8,128)}, f32[1,256,256]{2,1,0:T(8,128)}) async-done(((f32[1,256,256]{2,1,0:T(8,128)}, f32[1,256,256]{2,1,0:T(8,128)}), (f32[1,256,256]{2,1,0:T(8,128)}, f32[1,256,256]{2,1,0:T(8,128)})) %all-reduce.7.cloned.1.call-update) | async-done | bytes 524304 | tf_op jit(solution)/shard_map/psum | solution.py:26
  (120 shorter events, 77.5 us)
Async XLA Ops:
  43.5 53.8 %copy-start.5 = (f32[1,2,1,256,256]{4,3,2,1,0:T(8,128)S(1)}, f32[1,2,1,256,256]{4,3,2,1,0:T(8,128)}, u32[]{:S(2)}) copy-start(f32[1,2,1,256,256]{4,3,2,1,0:T(8,128)} %param.6) | copy-start | bytes 1572868
  43.5 22.6 %all-to-all-start.3 = ((f32[2,16,16,256]{3,2,0,1:T(8,128)}), f32[2,16,16,256]{3,2,0,1:T(8,128)S(1)}, u32[]{:S(2)}, u32[]{:S(2)}) async-start(f32[2,16,16,256]{3,2,0,1:T(8,128)} %broadcast_in_dim.91), calls=%async_computation.3 | async-start | bytes 1048576 | tf_op jit(solution)/shard_map/all_to_all | solution.py:46
  66.1 52.2 %copy-start = (f32[1,256,256]{2,1,0:T(8,128)S(1)}, f32[1,256,256]{2,1,0:T(8,128)}, u32[]{:S(2)}) copy-start(f32[1,256,256]{2,1,0:T(8,128)} %param.7) | copy-start | bytes 786436
  66.1 27.1 %all-to-all-start.1 = ((f32[32,16,256]{2,1,0:T(8,128)}), f32[32,16,256]{2,1,0:T(8,128)S(1)}, u32[]{:S(2)}, u32[]{:S(2)}) async-start(f32[32,16,256]{2,1,0:T(8,128)} %bitcast.5), calls=%async_computation.1 | async-start | bytes 1048576 | tf_op jit(solution)/shard_map/all_to_all | solution.py:56
  93.2 20.6 %all-to-all-start.4 = ((f32[32,16,256]{2,1,0:T(8,128)}), f32[32,16,256]{2,1,0:T(8,128)S(1)}, u32[]{:S(2)}, u32[]{:S(2)}) async-start(f32[32,16,256]{2,1,0:T(8,128)} %bitcast.12), calls=%async_computation.4 | async-start | bytes 1048576 | tf_op jit(solution)/shard_map/all_to_all | solution.py:56
  97.3 21.4 %collective-permute-start = (f32[2,256,256]{2,1,0:T(8,128)S(1)}, f32[2,256,256]{2,1,0:T(8,128)}, u32[]{:S(2)}, u32[]{:S(2)}) collective-permute-start(f32[2,256,256]{2,1,0:T(8,128)S(1)} %bitcast.230), channel_id=1, source_target_pairs={{0,1},{1,0},{2,3},{3,2},{4,5},{5,4},{6,7},{7,6},{8,9},{9,8},{10,11... | collective-permute-start | bytes 1572872 | tf_op jit(solution)/shard_map/ppermute | solution.py:15
  113.7 23.6 %all-to-all-start.2 = ((f32[2,16,16,256]{3,2,0,1:T(8,128)}), f32[2,16,16,256]{3,2,0,1:T(8,128)S(1)}, u32[]{:S(2)}, u32[]{:S(2)}) async-start(f32[2,16,16,256]{3,2,0,1:T(8,128)} %copy.27), calls=%async_computation.2 | async-start | bytes 1048576 | tf_op jit(solution)/shard_map/all_to_all | solution.py:46
  118.7 40.3 %collective-permute-start.1 = (f32[2,256,256]{2,1,0:T(8,128)}, f32[2,256,256]{2,1,0:T(8,128)}, u32[]{:S(2)}, u32[]{:S(2)}) collective-permute-start(f32[2,256,256]{2,1,0:T(8,128)} %collective-permute-done), channel_id=1, source_target_pairs={{0,2},{1,3},{2,0},{3,1},{4,6},{5,7},{6,4},{7,5},{8,10},{9,11},{10,... | collective-permute-start | bytes 1572872 | tf_op jit(solution)/shard_map/ppermute | solution.py:15
  124.1 67.4 %copy-start.4 = (f32[1,2,1,256,256]{4,3,2,1,0:T(8,128)S(1)}, f32[1,2,1,256,256]{4,3,2,1,0:T(8,128)}, u32[]{:S(2)}) copy-start(f32[1,2,1,256,256]{4,3,2,1,0:T(8,128)} %param.5) | copy-start | bytes 1572868
  137.4 54.8 %all-to-all-start.5 = ((f32[2,16,16,256]{3,2,0,1:T(8,128)}), f32[2,16,16,256]{3,2,0,1:T(8,128)S(1)}, u32[]{:S(2)}, u32[]{:S(2)}) async-start(f32[2,16,16,256]{3,2,0,1:T(8,128)} %copy.31), calls=%async_computation.5 | async-start | bytes 1048576 | tf_op jit(solution)/shard_map/all_to_all | solution.py:46
  143.1 341.7 %all-reduce.11.cloned.1.call-start = ((), (), s32[]{:S(2)}) async-start(), calls=%async_computation.14 | async-start | bytes 1048576 | tf_op jit(solution)/shard_map/psum | solution.py:26
  159.0 30.2 %collective-permute-start.2 = (f32[2,256,256]{2,1,0:T(8,128)}, f32[2,256,256]{2,1,0:T(8,128)}, u32[]{:S(2)}, u32[]{:S(2)}) collective-permute-start(f32[2,256,256]{2,1,0:T(8,128)} %collective-permute-done.1), channel_id=1, source_target_pairs={{0,4},{1,5},{2,6},{3,7},{4,0},{5,1},{6,2},{7,3},{8,12},{9,13},{10,... | collective-permute-start | bytes 1572872 | tf_op jit(solution)/shard_map/ppermute | solution.py:15
  189.3 23.4 %collective-permute-start.3 = (f32[2,256,256]{2,1,0:T(8,128)}, f32[2,256,256]{2,1,0:T(8,128)}, u32[]{:S(2)}, u32[]{:S(2)}) collective-permute-start(f32[2,256,256]{2,1,0:T(8,128)} %collective-permute-done.2), channel_id=1, source_target_pairs={{0,8},{1,9},{2,10},{3,11},{4,12},{5,13},{6,14},{7,15},{8,0},{9,1},... | collective-permute-start | bytes 1572872 | tf_op jit(solution)/shard_map/ppermute | solution.py:15
  196.1 3.3 copy-start.1
  537.5 24.0 %all-to-all-start.8 = ((f32[2,16,16,256]{3,2,0,1:T(8,128)}), f32[2,16,16,256]{3,2,0,1:T(8,128)S(1)}, u32[]{:S(2)}, u32[]{:S(2)}) async-start(f32[2,16,16,256]{3,2,0,1:T(8,128)} %copy.36), calls=%async_computation.8 | async-start | bytes 1048576 | tf_op jit(solution)/shard_map/all_to_all | solution.py:46
  542.4 307.6 %all-reduce.9.cloned.1.call-start = ((), (), s32[]{:S(2)}) async-start(), calls=%async_computation.13 | async-start | bytes 1048576 | tf_op jit(solution)/shard_map/psum | solution.py:26
  543.8 33.4 %collective-permute-start.4 = (f32[2,256,256]{2,1,0:T(8,128)}, f32[2,256,256]{2,1,0:T(8,128)}, u32[]{:S(2)}, u32[]{:S(2)}) collective-permute-start(f32[2,256,256]{2,1,0:T(8,128)} %collective-permute-done.3), channel_id=1, source_target_pairs={{1,0},{2,1},{3,2},{4,3},{5,4},{6,5},{7,6},{8,7},{9,8},{10,9},{11,1... | collective-permute-start | bytes 1572872 | tf_op jit(solution)/shard_map/ppermute | solution.py:21
  561.7 1.7 copy-start.2
  902.8 24.0 %all-to-all-start.11 = ((f32[2,16,16,256]{3,2,0,1:T(8,128)}), f32[2,16,16,256]{3,2,0,1:T(8,128)S(1)}, u32[]{:S(2)}, u32[]{:S(2)}) async-start(f32[2,16,16,256]{3,2,0,1:T(8,128)} %copy.41), calls=%async_computation.11 | async-start | bytes 1048576 | tf_op jit(solution)/shard_map/all_to_all | solution.py:46
  907.6 304.3 %all-reduce.7.cloned.1.call-start = ((), (), s32[]{:S(2)}) async-start(), calls=%async_computation.12 | async-start | bytes 1048576 | tf_op jit(solution)/shard_map/psum | solution.py:26
  909.0 35.8 %collective-permute-start.5 = (f32[2,256,256]{2,1,0:T(8,128)}, f32[2,256,256]{2,1,0:T(8,128)S(1)}, u32[]{:S(2)}, u32[]{:S(2)}) collective-permute-start(f32[2,256,256]{2,1,0:T(8,128)} %collective-permute-done.3), channel_id=1, source_target_pairs={{2,0},{3,1},{4,2},{5,3},{6,4},{7,5},{8,6},{9,7},{10,8},{11,9},{12,... | collective-permute-start | bytes 1572872 | tf_op jit(solution)/shard_map/ppermute | solution.py:21
  926.9 1.7 copy-start.3
Sparse Core Ops, SparseCore 0:
  200.8 283.9 all-reduce.10
  568.1 281.8 all-reduce.8
  933.3 278.5 all-reduce.6
where the time goes:
time: 1220 us
  waiting for transfers between devices  948 us (78%)
  blocking collectives  134 us (11%)
  starting transfers between devices  77.8 us (6%)
  matrix products  26.2 us (2%)
  between operations  17.7 us (1%)
  local copies, waits for them, and re-layouts  14.9 us (1%)
    psum x3, waiting for transfers between devices, spread(): return lax.psum(kept, axis)  807 us
    all_to_all x3, blocking collectives, across_cols(): lax.all_to_all(pieces, 'col', split_axis=1, concat_axis=1, tiled=True)  86.2 us
    all_to_all x2, blocking collectives, mirrored(): lax.all_to_all(by_target, 'row', split_axis=0, concat_axis=0, tiled=True)  47.8 us
    ppermute x4, waiting for transfers between devices, swapped(): return lax.ppermute(value, axis, pairs)  47.4 us
    all_to_all x5, waiting for transfers between devices, across_cols(): lax.all_to_all(pieces, 'col', split_axis=1, concat_axis=1, tiled=True)  44.9 us
    all_to_all x2, waiting for transfers between devices, mirrored(): lax.all_to_all(by_target, 'row', split_axis=0, concat_axis=0, tiled=True)  28 us
    all_to_all x5, starting transfers between devices, across_cols(): lax.all_to_all(pieces, 'col', split_axis=1, concat_axis=1, tiled=True)  25.6 us
  transfers between devices with their start and end apart: 16, of which 14 were waited for; matrix products, arithmetic and copies ran while one was open for 3% of the time, Pallas kernels for 0%

commit v1 on v0

--- a/solution.py
+++ b/solution.py
@@ -23,7 +23,8 @@
 
 def spread(value, axis, source):
     kept = jnp.where(lax.axis_index(axis) == source, value, 0).astype(value.dtype)
-    return lax.psum(kept, axis)
+    register_quotas_by_axis = lambda xin, axis_name: jnp.sum(lax.all_gather(xin, axis_name), axis=0)
+    return register_quotas_by_axis(kept, axis)
 
 
 def product(left, right):

time: 1220 us -> 834 us (0.68)
  waiting for transfers between devices: 948 us -> 540 us
  other arithmetic: 2.77 us -> 26.6 us
    psum x3 -> x0, waiting for transfers between devices: 807 us -> none  [spread(): return lax.psum(kept, axis)]
    all_gather x0 -> x6, waiting for transfers between devices: none -> 309 us  [spread(): lax.all_gather(xin, axis_name)]
    all_to_all x5, waiting for transfers between devices: 44.9 us -> 81.3 us  [across_cols(): lax.all_to_all(pieces, 'col', split_axis=1, concat_axis=1, tiled=True)]
    ppermute x4, waiting for transfers between devices: 47.4 us -> 79.2 us  [swapped(): return lax.ppermute(value, axis, pairs)]
    reduce_sum x0 -> x6, other arithmetic: none -> 26.4 us  [spread(): jnp.sum(lax.all_gather(xin, axis_name), axis=0)]
    ppermute x2, waiting for transfers between devices: 20.5 us -> 37.9 us  [passed_along(): return lax.ppermute(block, axis, route)]
  transfers between devices with their start and end apart: 16 -> 19, of which waited for: 14 -> 18; matrix products, arithmetic and copies ran while one was open for 3% -> 3% of each run, Pallas kernels for 0% -> 0%
where the time goes in v1:
time: 834 us; the launch traced here: 832 us
  waiting for transfers between devices  540 us (65%)
  blocking collectives  137 us (16%)
  starting transfers between devices  68.3 us (8%)
  matrix products  29.2 us (4%)
  other arithmetic  26.6 us (3%)
  between operations  18.3 us (2%)
  local copies, waits for them, and re-layouts  12.4 us (1%)
    all_gather x6, waiting for transfers between devices, spread(): lax.all_gather(xin, axis_name)  309 us
    all_to_all x3, blocking collectives, across_cols(): lax.all_to_all(pieces, 'col', split_axis=1, concat_axis=1, tiled=True)  89.2 us
    all_to_all x5, waiting for transfers between devices, across_cols(): lax.all_to_all(pieces, 'col', split_axis=1, concat_axis=1, tiled=True)  81.3 us
    ppermute x4, waiting for transfers between devices, swapped(): return lax.ppermute(value, axis, pairs)  79.2 us
    all_to_all x2, blocking collectives, mirrored(): lax.all_to_all(by_target, 'row', split_axis=0, concat_axis=0, tiled=True)  48.1 us
    ppermute x2, waiting for transfers between devices, passed_along(): return lax.ppermute(block, axis, route)  37.9 us
    all_to_all x2, waiting for transfers between devices, mirrored(): lax.all_to_all(by_target, 'row', split_axis=0, concat_axis=0, tiled=True)  31.1 us
    reduce_sum x6, other arithmetic, spread(): jnp.sum(lax.all_gather(xin, axis_name), axis=0)  26.4 us
  transfers between devices with their start and end apart: 19, of which 18 were waited for; matrix products, arithmetic and copies ran while one was open for 3% of the time, Pallas kernels for 0%

profile of v1, /device:TPU:1, one launch (start us, length us, event | category | flops | bytes accessed | tf_op | source)
XLA Modules:
  0.0 832.2 jit_solution(12870317490297075241)
XLA Ops:
  7.6 34.1 %all_to_all.60 = f32[2,16,16,256]{3,2,0,1:T(8,128)S(1)} all-to-all(f32[2,16,16,256]{3,2,0,1:T(8,128)S(1)} %copy.25), channel_id=1, replica_groups=mesh['row'=32,'col'=16] {'col'}, dimensions={1} | all-to-all | bytes 1048576 | tf_op jit(solution)/shard_map/all_to_all | solution.py:47
  49.9 16.1 %all-to-all-done.3 = f32[2,16,16,256]{3,2,0,1:T(8,128)S(1)} async-done(((f32[2,16,16,256]{3,2,0,1:T(8,128)}), f32[2,16,16,256]{3,2,0,1:T(8,128)S(1)}, u32[]{:S(2)}, u32[]{:S(2)}) %all-to-all-start.3) | async-done | bytes 524320 | tf_op jit(solution)/shard_map/all_to_all | solution.py:47
  66.0 10.6 %all-to-all-start.1 = ((f32[32,16,256]{2,1,0:T(8,128)}), f32[32,16,256]{2,1,0:T(8,128)S(1)}, u32[]{:S(2)}, u32[]{:S(2)}) async-start(f32[32,16,256]{2,1,0:T(8,128)} %bitcast.5), calls=%async_computation.1 | async-start | bytes 1048576 | tf_op jit(solution)/shard_map/all_to_all | solution.py:57
  77.5 15.6 %all-to-all-done.1 = f32[32,16,256]{2,1,0:T(8,128)S(1)} async-done(((f32[32,16,256]{2,1,0:T(8,128)}), f32[32,16,256]{2,1,0:T(8,128)S(1)}, u32[]{:S(2)}, u32[]{:S(2)}) %all-to-all-start.1) | async-done | bytes 524320 | tf_op jit(solution)/shard_map/all_to_all | solution.py:57
  98.1 15.6 %all-to-all-done.4 = f32[32,16,256]{2,1,0:T(8,128)S(1)} async-done(((f32[32,16,256]{2,1,0:T(8,128)}), f32[32,16,256]{2,1,0:T(8,128)S(1)}, u32[]{:S(2)}, u32[]{:S(2)}) %all-to-all-start.4) | async-done | bytes 524320 | tf_op jit(solution)/shard_map/all_to_all | solution.py:57
  119.8 17.4 %all-to-all-done.2 = f32[2,16,16,256]{3,2,0,1:T(8,128)S(1)} async-done(((f32[2,16,16,256]{3,2,0,1:T(8,128)}), f32[2,16,16,256]{3,2,0,1:T(8,128)S(1)}, u32[]{:S(2)}, u32[]{:S(2)}) %all-to-all-start.2) | async-done | bytes 524320 | tf_op jit(solution)/shard_map/all_to_all | solution.py:47
  147.1 12.7 %all-to-all-done.5 = f32[2,16,16,256]{3,2,0,1:T(8,128)S(1)} async-done(((f32[2,16,16,256]{3,2,0,1:T(8,128)}), f32[2,16,16,256]{3,2,0,1:T(8,128)S(1)}, u32[]{:S(2)}, u32[]{:S(2)}) %all-to-all-start.5) | async-done | bytes 524320 | tf_op jit(solution)/shard_map/all_to_all | solution.py:47
  186.0 22.6 %collective-permute-done.1 = f32[2,256,256]{2,1,0:T(8,128)S(1)} collective-permute-done((f32[2,256,256]{2,1,0:T(8,128)S(1)}, f32[2,256,256]{2,1,0:T(8,128)S(1)}, u32[]{:S(2)}, u32[]{:S(2)}) %collective-permute-start.1) | collective-permute-done | bytes 524320 | tf_op jit(solution)/shard_map/ppermute | solution.py:15
  208.7 9.2 %collective-permute-start.2 = (f32[2,256,256]{2,1,0:T(8,128)S(1)}, f32[2,256,256]{2,1,0:T(8,128)S(1)}, u32[]{:S(2)}, u32[]{:S(2)}) collective-permute-start(f32[2,256,256]{2,1,0:T(8,128)S(1)} %collective-permute-done.1), channel_id=1, source_target_pairs={{0,4},{1,5},{2,6},{3,7},{4,0},{5,1},{6,2},{7,3},{8,12},{9,13},{10,... | collective-permute-start | bytes 1572872 | tf_op jit(solution)/shard_map/ppermute | solution.py:15
  217.9 23.1 %collective-permute-done.2 = f32[2,256,256]{2,1,0:T(8,128)S(1)} collective-permute-done((f32[2,256,256]{2,1,0:T(8,128)S(1)}, f32[2,256,256]{2,1,0:T(8,128)S(1)}, u32[]{:S(2)}, u32[]{:S(2)}) %collective-permute-start.2) | collective-permute-done | bytes 524320 | tf_op jit(solution)/shard_map/ppermute | solution.py:15
  244.0 24.4 %collective-permute-done.3 = f32[2,256,256]{2,1,0:T(8,128)S(1)} collective-permute-done((f32[2,256,256]{2,1,0:T(8,128)S(1)}, f32[2,256,256]{2,1,0:T(8,128)S(1)}, u32[]{:S(2)}, u32[]{:S(2)}) %collective-permute-start.3) | collective-permute-done | bytes 524320 | tf_op jit(solution)/shard_map/ppermute | solution.py:15
  273.7 57.1 %all-gather.15.cloned.1.call-done = f32[8192,256]{1,0:T(8,128)} async-done(((f32[256,256]{1,0:T(8,128)}), f32[8192,256]{1,0:T(8,128)}) %all-gather.15.cloned.1.call-update) | async-done | bytes 8388624 | tf_op jit(solution)/shard_map/all_gather | solution.py:26
  337.3 27.6 %all_to_all.61 = f32[2,16,16,256]{3,2,0,1:T(8,128)S(1)} all-to-all(f32[2,16,16,256]{3,2,0,1:T(8,128)S(1)} %copy.34), channel_id=1, replica_groups=mesh['row'=32,'col'=16] {'col'}, dimensions={1} | all-to-all | bytes 1048576 | tf_op jit(solution)/shard_map/all_to_all | solution.py:47
  364.9 24.1 %all_to_all.62 = f32[32,16,256]{2,1,0:T(8,128)S(1)} all-to-all(f32[32,16,256]{2,1,0:T(8,128)S(1)} %bitcast.235), channel_id=1, replica_groups=mesh['row'=32,'col'=16] {'row'}, dimensions={0} | all-to-all | bytes 1048576 | tf_op jit(solution)/shard_map/all_to_all | solution.py:57
  395.7 17.7 %all-to-all-done.8 = f32[2,16,16,256]{3,2,0,1:T(8,128)S(1)} async-done(((f32[2,16,16,256]{3,2,0,1:T(8,128)}), f32[2,16,16,256]{3,2,0,1:T(8,128)S(1)}, u32[]{:S(2)}, u32[]{:S(2)}) %all-to-all-start.8) | async-done | bytes 524320 | tf_op jit(solution)/shard_map/all_to_all | solution.py:47
  424.7 16.2 %collective-permute-done.4 = f32[2,256,256]{2,1,0:T(8,128)} collective-permute-done((f32[2,256,256]{2,1,0:T(8,128)S(1)}, f32[2,256,256]{2,1,0:T(8,128)}, u32[]{:S(2)}, u32[]{:S(2)}) %collective-permute-start.4) | collective-permute-done | bytes 524320 | tf_op jit(solution)/shard_map/ppermute | solution.py:21
  442.5 43.1 %all-gather.17.cloned.1.call-done = f32[8192,256]{1,0:T(8,128)} async-done(((f32[256,256]{1,0:T(8,128)}), f32[8192,256]{1,0:T(8,128)}) %all-gather.17.cloned.1.call-update) | async-done | bytes 8388624 | tf_op jit(solution)/shard_map/all_gather | solution.py:26
  490.3 84.1 %all-gather.19.cloned.1.call-done = f32[8192,256]{1,0:T(8,128)} async-done(((f32[256,256]{1,0:T(8,128)}), f32[8192,256]{1,0:T(8,128)}) %all-gather.19.cloned.1.call-update) | async-done | bytes 8388624 | tf_op jit(solution)/shard_map/all_gather | solution.py:26
  580.9 27.6 %all_to_all.63 = f32[2,16,16,256]{3,2,0,1:T(8,128)S(1)} all-to-all(f32[2,16,16,256]{3,2,0,1:T(8,128)S(1)} %copy.39), channel_id=1, replica_groups=mesh['row'=32,'col'=16] {'col'}, dimensions={1} | all-to-all | bytes 1048576 | tf_op jit(solution)/shard_map/all_to_all | solution.py:47
  608.5 24.1 %all_to_all.64 = f32[32,16,256]{2,1,0:T(8,128)S(1)} all-to-all(f32[32,16,256]{2,1,0:T(8,128)S(1)} %bitcast.237), channel_id=1, replica_groups=mesh['row'=32,'col'=16] {'row'}, dimensions={0} | all-to-all | bytes 1048576 | tf_op jit(solution)/shard_map/all_to_all | solution.py:57
  639.6 17.4 %all-to-all-done.11 = f32[2,16,16,256]{3,2,0,1:T(8,128)S(1)} async-done(((f32[2,16,16,256]{3,2,0,1:T(8,128)}), f32[2,16,16,256]{3,2,0,1:T(8,128)S(1)}, u32[]{:S(2)}, u32[]{:S(2)}) %all-to-all-start.11) | async-done | bytes 524320 | tf_op jit(solution)/shard_map/all_to_all | solution.py:47
  669.4 21.7 %collective-permute-done.5 = f32[2,256,256]{2,1,0:T(8,128)S(1)} collective-permute-done((f32[2,256,256]{2,1,0:T(8,128)S(1)}, f32[2,256,256]{2,1,0:T(8,128)S(1)}, u32[]{:S(2)}, u32[]{:S(2)}) %collective-permute-start.5) | collective-permute-done | bytes 524320 | tf_op jit(solution)/shard_map/ppermute | solution.py:21
  691.7 37.5 %all-gather.21.cloned.1.call-done = f32[8192,256]{1,0:T(8,128)} async-done(((f32[256,256]{1,0:T(8,128)}), f32[8192,256]{1,0:T(8,128)}) %all-gather.21.cloned.1.call-update) | async-done | bytes 8388624 | tf_op jit(solution)/shard_map/all_gather | solution.py:26
  733.2 86.8 %all-gather.23.cloned.1.call-done = f32[8192,256]{1,0:T(8,128)} async-done(((f32[256,256]{1,0:T(8,128)}), f32[8192,256]{1,0:T(8,128)}) %all-gather.23.cloned.1.call-update) | async-done | bytes 8388624 | tf_op jit(solution)/shard_map/all_gather | solution.py:26
  (138 shorter events, 127.6 us)
Async XLA Ops:
  43.5 22.5 %all-to-all-start.3 = ((f32[2,16,16,256]{3,2,0,1:T(8,128)}), f32[2,16,16,256]{3,2,0,1:T(8,128)S(1)}, u32[]{:S(2)}, u32[]{:S(2)}) async-start(f32[2,16,16,256]{3,2,0,1:T(8,128)} %broadcast_in_dim.91), calls=%async_computation.3 | async-start | bytes 1048576 | tf_op jit(solution)/shard_map/all_to_all | solution.py:47
  66.0 52.2 %copy-start = (f32[1,256,256]{2,1,0:T(8,128)S(1)}, f32[1,256,256]{2,1,0:T(8,128)}, u32[]{:S(2)}) copy-start(f32[1,256,256]{2,1,0:T(8,128)} %param.7) | copy-start | bytes 786436
  66.0 27.1 %all-to-all-start.1 = ((f32[32,16,256]{2,1,0:T(8,128)}), f32[32,16,256]{2,1,0:T(8,128)S(1)}, u32[]{:S(2)}, u32[]{:S(2)}) async-start(f32[32,16,256]{2,1,0:T(8,128)} %bitcast.5), calls=%async_computation.1 | async-start | bytes 1048576 | tf_op jit(solution)/shard_map/all_to_all | solution.py:57
  93.1 20.6 %all-to-all-start.4 = ((f32[32,16,256]{2,1,0:T(8,128)}), f32[32,16,256]{2,1,0:T(8,128)S(1)}, u32[]{:S(2)}, u32[]{:S(2)}) async-start(f32[32,16,256]{2,1,0:T(8,128)} %bitcast.12), calls=%async_computation.4 | async-start | bytes 1048576 | tf_op jit(solution)/shard_map/all_to_all | solution.py:57
  113.6 23.6 %all-to-all-start.2 = ((f32[2,16,16,256]{3,2,0,1:T(8,128)}), f32[2,16,16,256]{3,2,0,1:T(8,128)S(1)}, u32[]{:S(2)}, u32[]{:S(2)}) async-start(f32[2,16,16,256]{3,2,0,1:T(8,128)} %copy.27), calls=%async_computation.2 | async-start | bytes 1048576 | tf_op jit(solution)/shard_map/all_to_all | solution.py:47
  119.8 26.0 %copy-start.4 = (f32[1,2,1,256,256]{4,3,2,1,0:T(8,128)S(1)}, f32[1,2,1,256,256]{4,3,2,1,0:T(8,128)}, u32[]{:S(2)}) copy-start(f32[1,2,1,256,256]{4,3,2,1,0:T(8,128)} %param.5) | copy-start | bytes 1572868
  137.3 22.5 %all-to-all-start.5 = ((f32[2,16,16,256]{3,2,0,1:T(8,128)}), f32[2,16,16,256]{3,2,0,1:T(8,128)S(1)}, u32[]{:S(2)}, u32[]{:S(2)}) async-start(f32[2,16,16,256]{3,2,0,1:T(8,128)} %copy.31), calls=%async_computation.5 | async-start | bytes 1048576 | tf_op jit(solution)/shard_map/all_to_all | solution.py:47
  142.5 126.5 %all-gather.13.cloned.1.call-start = ((), (), s32[]{:S(2)}) async-start(), calls=%async_computation.12 | async-start | bytes 8650752 | tf_op jit(solution)/shard_map/all_gather | solution.py:26
  164.6 3.3 copy-start.1
  166.7 3.3 copy-start.8
  169.2 161.6 %all-gather.15.cloned.1.call-start = ((), (), s32[]{:S(2)}) async-start(), calls=%async_computation.13 | async-start | bytes 8650752 | tf_op jit(solution)/shard_map/all_gather | solution.py:26
  170.0 12.6 %collective-permute-start = (f32[2,256,256]{2,1,0:T(8,128)S(1)}, f32[2,256,256]{2,1,0:T(8,128)S(1)}, u32[]{:S(2)}, u32[]{:S(2)}) collective-permute-start(f32[2,256,256]{2,1,0:T(8,128)S(1)} %bitcast.248), channel_id=1, source_target_pairs={{0,1},{1,0},{2,3},{3,2},{4,5},{5,4},{6,7},{7,6},{8,9},{9,8},{10,11... | collective-permute-start | bytes 1572872 | tf_op jit(solution)/shard_map/ppermute | solution.py:15
  182.6 26.1 %collective-permute-start.1 = (f32[2,256,256]{2,1,0:T(8,128)S(1)}, f32[2,256,256]{2,1,0:T(8,128)S(1)}, u32[]{:S(2)}, u32[]{:S(2)}) collective-permute-start(f32[2,256,256]{2,1,0:T(8,128)S(1)} %collective-permute-done), channel_id=1, source_target_pairs={{0,2},{1,3},{2,0},{3,1},{4,6},{5,7},{6,4},{7,5},{8,10},{9,11},{10,... | collective-permute-start | bytes 1572872 | tf_op jit(solution)/shard_map/ppermute | solution.py:15
  208.7 32.3 %collective-permute-start.2 = (f32[2,256,256]{2,1,0:T(8,128)S(1)}, f32[2,256,256]{2,1,0:T(8,128)S(1)}, u32[]{:S(2)}, u32[]{:S(2)}) collective-permute-start(f32[2,256,256]{2,1,0:T(8,128)S(1)} %collective-permute-done.1), channel_id=1, source_target_pairs={{0,4},{1,5},{2,6},{3,7},{4,0},{5,1},{6,2},{7,3},{8,12},{9,13},{10,... | collective-permute-start | bytes 1572872 | tf_op jit(solution)/shard_map/ppermute | solution.py:15
  241.0 27.4 %collective-permute-start.3 = (f32[2,256,256]{2,1,0:T(8,128)S(1)}, f32[2,256,256]{2,1,0:T(8,128)S(1)}, u32[]{:S(2)}, u32[]{:S(2)}) collective-permute-start(f32[2,256,256]{2,1,0:T(8,128)S(1)} %collective-permute-done.2), channel_id=1, source_target_pairs={{0,8},{1,9},{2,10},{3,11},{4,12},{5,13},{6,14},{7,15},{8,0},{9,1},... | collective-permute-start | bytes 1572872 | tf_op jit(solution)/shard_map/ppermute | solution.py:15
  268.4 5.3 copy-start.5
  389.8 23.6 %all-to-all-start.8 = ((f32[2,16,16,256]{3,2,0,1:T(8,128)}), f32[2,16,16,256]{3,2,0,1:T(8,128)S(1)}, u32[]{:S(2)}, u32[]{:S(2)}) async-start(f32[2,16,16,256]{3,2,0,1:T(8,128)} %copy.36), calls=%async_computation.8 | async-start | bytes 1048576 | tf_op jit(solution)/shard_map/all_to_all | solution.py:47
  394.3 91.4 %all-gather.17.cloned.1.call-start = ((), (), s32[]{:S(2)}) async-start(), calls=%async_computation.14 | async-start | bytes 8650752 | tf_op jit(solution)/shard_map/all_gather | solution.py:26
  420.0 154.5 %all-gather.19.cloned.1.call-start = ((), (), s32[]{:S(2)}) async-start(), calls=%async_computation.15 | async-start | bytes 8650752 | tf_op jit(solution)/shard_map/all_gather | solution.py:26
  420.5 20.3 %collective-permute-start.4 = (f32[2,256,256]{2,1,0:T(8,128)S(1)}, f32[2,256,256]{2,1,0:T(8,128)}, u32[]{:S(2)}, u32[]{:S(2)}) collective-permute-start(f32[2,256,256]{2,1,0:T(8,128)S(1)} %copy-done.6), channel_id=1, source_target_pairs={{1,0},{2,1},{3,2},{4,3},{5,4},{6,5},{7,6},{8,7},{9,8},{10,9},{11,1... | collective-permute-start | bytes 1572872 | tf_op jit(solution)/shard_map/ppermute | solution.py:21
  633.4 23.6 %all-to-all-start.11 = ((f32[2,16,16,256]{3,2,0,1:T(8,128)}), f32[2,16,16,256]{3,2,0,1:T(8,128)S(1)}, u32[]{:S(2)}, u32[]{:S(2)}) async-start(f32[2,16,16,256]{3,2,0,1:T(8,128)} %copy.41), calls=%async_computation.11 | async-start | bytes 1048576 | tf_op jit(solution)/shard_map/all_to_all | solution.py:47
  638.0 91.3 %all-gather.21.cloned.1.call-start = ((), (), s32[]{:S(2)}) async-start(), calls=%async_computation.16 | async-start | bytes 8650752 | tf_op jit(solution)/shard_map/all_gather | solution.py:26
  663.5 156.4 %all-gather.23.cloned.1.call-start = ((), (), s32[]{:S(2)}) async-start(), calls=%async_computation.17 | async-start | bytes 8650752 | tf_op jit(solution)/shard_map/all_gather | solution.py:26
  664.1 27.0 %collective-permute-start.5 = (f32[2,256,256]{2,1,0:T(8,128)S(1)}, f32[2,256,256]{2,1,0:T(8,128)S(1)}, u32[]{:S(2)}, u32[]{:S(2)}) collective-permute-start(f32[2,256,256]{2,1,0:T(8,128)S(1)} %copy-done.7), channel_id=1, source_target_pairs={{2,0},{3,1},{4,2},{5,3},{6,4},{7,5},{8,6},{9,7},{10,8},{11,9},{12,... | collective-permute-start | bytes 1572872 | tf_op jit(solution)/shard_map/ppermute | solution.py:21
  (4 other events, 9.6 us)
Sparse Core Ops, SparseCore 0:
  169.3 67.7 all-gather.12
  239.3 91.3 all-gather.14
  420.1 65.5 all-gather.16
  487.7 86.7 all-gather.18
  663.6 65.5 all-gather.20
  731.2 88.6 all-gather.22
